TPU v7x, 512 devices: a whole 4x4x16 slice. The times are simulated.
512 devices in a mesh: pulse: 4 (over z_lo), range: 4 (over y), tile: 32 (over z_hi, x, core).
Axes of the slice: x: 4, y: 4, z: 16 (z_hi: 4, z_lo: 4; z = z_hi * 4 + z_lo), core: 2. Of those that a mesh axis runs over, the one named last changes fastest.
Arguments:
- echo: bfloat16 [2, 1024, 32768], P(None, ('pulse', 'tile'), 'range'), may hold values from -6 to 6
- replica: bfloat16 [2, 4096], replicated, may hold values from -0.09375 to 0.09375
- interp: bfloat16 [32, 256, 128], P('range'), may hold values from -0.375 to 0.375
- band_start: int32 [1024, 32, 4], P(('pulse', 'tile'), None, 'range'), may hold values from 0 to 7040, as said below
- visible: int32 [1024, 32], P(('pulse', 'tile')), may hold values 0 or 1
- doppler: int32 [1024], P(('pulse', 'tile')), may hold values from 0 to 8191
- range_step: int32 [1024], P(('pulse', 'tile')), may hold values from 0 to 4095
Outputs:
- image: float32 [2, 8192, 4096], P(None, ('tile', 'pulse'), 'range')
Inputs may be any that keep to these rules, and one draw needn't show every extreme that they name: band_start is counted within the 8192 bins of range block b and is a multiple of 128; the values 0 and 7040 both occur.
All inputs are finite; a program needn't handle non-finite values. No bound on the sum of `visible` on one device may be relied on, other than what follows from the above.
Results may differ from a plain program's by a relative error of at most 0.0047.
Values may be sent and summed in bfloat16 or wider, within the bound.
No kernel may reach another device: no remote copies, remote signals or barrier semaphores. Data moves between devices by JAX's collectives and lax.ppermute only.
A program may use at most 64 MiB of HBM per device.

v0:
```python
import math
import jax
import jax.numpy as jnp
from jax import lax
from jax.sharding import PartitionSpec as P

AZ_DEV = 64


def padded_2(cells, sides, width):
    for axis, dim in sides:
        count = lax.axis_size(axis)
        ends = count - 1
        head = lax.slice_in_dim(cells, 0, width, axis=dim)
        tail = lax.slice_in_dim(cells, cells.shape[dim] - width, cells.shape[dim], axis=dim)
        cells = jnp.concatenate(
            [
                lax.ppermute(tail, axis, [(i, (i + 1) % count) for i in range(ends)]),
                cells,
                lax.ppermute(head, axis, [((i + 1) % count, i) for i in range(ends)]),
            ],
            axis=dim,
        )
    return cells


def toeplitz_block(padded, offset, block_width):
    segment = lax.dynamic_slice_in_dim(padded, offset, 2 * block_width + 1)
    repeated = jnp.tile(segment, block_width)[: 2 * block_width * block_width]
    skewed = repeated.reshape(block_width, 2 * block_width)
    return skewed[:, block_width:].T


def chirp_matrix(padded_real, padded_imag, offset, block_width):
    toep_real = toeplitz_block(padded_real, offset, block_width)
    toep_imag = toeplitz_block(padded_imag, offset, block_width)
    upper_rows = jnp.concatenate([toep_real, -toep_imag], axis=1)
    lower_rows = jnp.concatenate([toep_imag, toep_real], axis=1)
    return jnp.concatenate([upper_rows, lower_rows], axis=0)


def compress(extended, replica, block_width):
    chirp_len = replica.shape[1]
    pulses = extended.shape[1]
    total_blocks = extended.shape[2] // block_width
    out_blocks = total_blocks - chirp_len // block_width
    arranged = extended.reshape(2, pulses, total_blocks, block_width).transpose(1, 2, 0, 3)
    margin = jnp.zeros((2, block_width), replica.dtype)
    padded = jnp.concatenate([margin, replica, margin, margin[:, :1]], axis=1)

    def add_turn(turn_index, running):
        offset = (turn_index * block_width).astype(jnp.int32)
        matrix = chirp_matrix(padded[0], padded[1], offset, block_width)
        window = lax.dynamic_slice_in_dim(arranged, turn_index.astype(jnp.int32), out_blocks, 1)
        window = window.reshape(pulses * out_blocks, 2 * block_width)
        return running + jnp.dot(window, matrix, preferred_element_type=jnp.float32)

    start_total = jnp.zeros((pulses * out_blocks, 2 * block_width), jnp.float32)
    running = lax.fori_loop(0, chirp_len // block_width + 1, add_turn, start_total)
    shaped = running.reshape(pulses, out_blocks, 2, block_width).transpose(0, 2, 1, 3)
    return shaped.reshape(pulses, 2, out_blocks * block_width).astype(jnp.bfloat16)


def select_bands(signals, first_bins, band_len, line_block):
    pulses = signals.shape[0]
    block_total = signals.shape[2] // line_block
    band_blocks = band_len // line_block
    pieces = signals.reshape(pulses, 2, block_total, line_block)
    wanted = first_bins[:, None] // line_block + jnp.arange(band_blocks, dtype=jnp.int32)[None, :]
    chooser = (
        wanted[:, :, None] == jnp.arange(block_total, dtype=jnp.int32)[None, None, :]
    ).astype(jnp.bfloat16)
    picked = jnp.einsum("pjk,pckl->pcjl", chooser, pieces, preferred_element_type=jnp.float32)
    return picked.astype(jnp.bfloat16).reshape(pulses, 2, band_len)


def steer_lines(band_rows, interp_block, range_steps, first_line, range_total):
    pulses = band_rows.shape[0]
    block_count = interp_block.shape[0]
    line_block = interp_block.shape[2]
    pieces = band_rows.reshape(pulses, 2, block_count + 1, line_block)
    windows = jnp.concatenate([pieces[:, :, :-1], pieces[:, :, 1:]], axis=3)
    line_values = jnp.einsum(
        "pcjb,jbl->pcjl", windows, interp_block, preferred_element_type=jnp.float32
    )
    line_values = line_values.reshape(pulses, 2, block_count * line_block)
    line_number = first_line + jnp.arange(block_count * line_block, dtype=jnp.int32)
    phase_turns = range_steps[:, None] * line_number[None, :] % range_total
    phase_angle = phase_turns.astype(jnp.float32) * (2.0 * math.pi / range_total)
    cosine = jnp.cos(phase_angle)
    sine_part = jnp.sin(phase_angle)
    steered_real = line_values[:, 0] * cosine - line_values[:, 1] * sine_part
    steered_imag = line_values[:, 0] * sine_part + line_values[:, 1] * cosine
    return jnp.stack([steered_real, steered_imag], axis=1).astype(jnp.bfloat16)


def azimuth_factor(doppler_bins, visible_flags, line_number, azimuth_total, norm_scale):
    phase_turns = line_number[:, None] * doppler_bins[None, :] % azimuth_total
    phase_angle = phase_turns.astype(jnp.float32) * (2.0 * math.pi / azimuth_total)
    weight = visible_flags.astype(jnp.float32)[None, :] * norm_scale
    factor_real = (jnp.cos(phase_angle) * weight).astype(jnp.bfloat16)
    factor_imag = (jnp.sin(phase_angle) * weight).astype(jnp.bfloat16)
    return (factor_real, factor_imag)


def add_pulses(factor_real, factor_imag, steered):
    left_side = jnp.concatenate([factor_real, factor_imag], axis=1)
    steer_real = steered[:, 0]
    steer_imag = steered[:, 1]
    top_rows = jnp.concatenate([steer_real, steer_imag], axis=1)
    bottom_rows = jnp.concatenate([-steer_imag, steer_real], axis=1)
    right_side = jnp.concatenate([top_rows, bottom_rows], axis=0)
    return jnp.dot(left_side, right_side, preferred_element_type=jnp.float32)


def local(echo, replica, interp, band_start, visible, doppler, range_step):
    chirp_len = replica.shape[1]
    half_chirp = chirp_len // 2
    block_width = min(256, half_chirp)
    pulses_dev = echo.shape[1]
    line_block = interp.shape[2]
    lines_dev = interp.shape[0] * line_block
    band_len = lines_dev + line_block
    tile_count = lax.axis_size("tile")
    pulse_count = lax.axis_size("pulse")
    range_total = lines_dev * lax.axis_size("range")
    azimuth_total = AZ_DEV * pulse_count * tile_count
    group_pulses = pulses_dev * tile_count
    norm_scale = (pulses_dev * pulse_count * tile_count) ** (-0.5)
    tile_number = lax.axis_index("tile")
    first_line = lax.axis_index("range") * lines_dev
    extended = padded_2(echo, (("range", 2),), half_chirp)
    compressed = compress(extended, replica, block_width)
    empty_index = jnp.zeros((group_pulses,), jnp.int32)
    first_row = jnp.int32(0)
    signals = lax.all_gather(compressed, "tile", axis=0, tiled=True)
    starts_in = lax.all_gather(band_start, "tile", axis=0, tiled=True)
    flags_in = lax.all_gather(visible, "tile", axis=0, tiled=True)
    doppler_in = lax.all_gather(doppler, "tile", axis=0, tiled=True)
    steps_in = lax.all_gather(range_step, "tile", axis=0, tiled=True)
    first_bins = lax.dynamic_index_in_dim(starts_in[:, :, 0], tile_number, 1, keepdims=False)
    flags_tile = lax.dynamic_index_in_dim(flags_in, tile_number, 1, keepdims=False)
    band_rows = select_bands(signals, first_bins, band_len, line_block)
    steered_in = steer_lines(band_rows, interp, steps_in, first_line, range_total)
    doppler_all = lax.dynamic_update_slice_in_dim(empty_index, doppler_in, first_row, 0)
    flags_all = lax.dynamic_update_slice_in_dim(empty_index, flags_tile, first_row, 0)
    tile_first = tile_number * (pulse_count * AZ_DEV)
    strip_lines = tile_first + jnp.arange(pulse_count * AZ_DEV, dtype=jnp.int32)
    factor_real, factor_imag = azimuth_factor(
        doppler_all, flags_all, strip_lines, azimuth_total, norm_scale
    )
    partial_image = add_pulses(factor_real, factor_imag, steered_in)
    image_rows = lax.psum_scatter(partial_image, "pulse", scatter_dimension=0, tiled=True)
    return image_rows.reshape(AZ_DEV, 2, lines_dev).transpose(1, 0, 2)


def solution(mesh):
    in_specs = (
        P(None, ("pulse", "tile"), "range"),
        P(),
        P("range", None, None),
        P(("pulse", "tile"), None, "range"),
        P(("pulse", "tile"), None),
        P(("pulse", "tile")),
        P(("pulse", "tile")),
    )
    out_specs = P(None, ("tile", "pulse"), "range")
    return jax.shard_map(local, mesh=mesh, in_specs=in_specs, out_specs=out_specs, check_vma=False)
```

profile of v0, /device:TPU:1, one launch (start us, length us, event | category | flops | bytes accessed | tf_op | source)
XLA Modules:
  0.0 323.4 jit_solution(15231582714423784350)
XLA Ops:
  6.5 0.9 fusion.47
  7.5 1.3 collective-permute-start.1
  8.8 4.7 %collective-permute-start = (bf16[2,8,2048]{2,1,0:T(8,128)(2,1)S(1)}, bf16[2,8,2048]{2,1,0:T(8,128)(2,1)S(1)}, u32[]{:S(2)}, u32[]{:S(2)}) collective-permute-start(bf16[2,8,2048]{2,1,0:T(8,128)(2,1)S(1)} %get-tuple-element.126), channel_id=1, source_target_pairs={{0,32},{32,64},{64,96},{1,33},{33,65},{65,97},{2,34},{34,66},{66,9... | collective-permute-start | bytes 196616 | tf_op jit(solution)/shard_map/ppermute | solution.py:18
  13.5 0.7 maximum_maximum_fusion
  14.8 1.0 pad_maximum_fusion.1
  15.8 45.2 %while.14 = (s32[]{:T(128)}, f32[256,512]{1,0:T(8,128)S(1)}, bf16[8,48,2,256]{3,1,0,2:T(8,128)(2,1)S(1)}, bf16[2,4609]{1,0:T(2,128)(2,1)S(1)}, s32[]{:T(128)}, /*index=5*/s32[]{:T(128)}, s32[]{:T(128)}, s32[]{:T(128)}) while((s32[]{:T(128)}, f32[256,512]{1,0:T(8,128)S(1)}, bf16[8,48,2,256]{3,1,0,2:T(8,128)(2,1)S(1)}, ...), condition=%wide.region_1.0_spmd.clone, body=%wide.region_0.0_spmd.clone.sunk | while | flops 136642560 | bytes 7779505 | solution.py:59
  16.4 0.6 tile.65
  17.2 0.6 tile.67
  19.0 0.6 tile.65
  19.9 0.6 tile.67
  21.7 0.6 tile.65
  22.6 0.6 tile.67
  24.4 0.6 tile.65
  25.2 0.6 tile.67
  27.0 0.6 tile.65
  27.9 0.6 tile.67
  29.7 0.6 tile.65
  30.5 0.6 tile.67
  32.3 0.6 tile.65
  33.2 0.6 tile.67
  35.0 0.6 tile.65
  35.9 0.6 tile.67
  37.7 0.6 tile.65
  38.5 0.6 tile.67
  40.3 0.6 tile.65
  45.6 0.6 tile.65
  48.3 0.6 tile.65
  51.0 0.6 tile.65
  51.8 0.6 tile.67
  53.6 0.6 tile.65
  54.5 0.6 tile.67
  57.1 0.6 tile.67
  59.8 0.6 tile.67
  61.3 0.8 convert_element_type.58
  62.1 1.2 dynamic-slice.7
  64.4 26.6 %all-reduce.2 = (s32[256]{0:T(256)S(1)}, s32[256]{0:T(256)S(1)}) all-reduce(s32[256]{0:T(256)S(1)} %dynamic-update-slice.1, s32[256]{0:T(256)S(1)} %dynamic-update-slice), channel_id=1, replica_groups=mesh['pulse'=4,'range'=4,'tile'=32] {'tile'}, use_global_device_ids=true, to_apply=%add.1 | all-reduce | flops 512 | bytes 4096
  91.0 53.7 %all_gather.16 = s32[256,32]{1,0:T(8,128)S(1)} all-gather(s32[8,32]{1,0:T(8,128)S(1)} %copy-done.1), channel_id=1, replica_groups=mesh['pulse'=4,'range'=4,'tile'=32] {'tile'}, dimensions={0}, use_global_device_ids=true | all-gather | bytes 33792 | tf_op jit(solution)/shard_map/all_gather | solution.py:138
  144.9 74.4 %all_gather.18 = s32[256,32,1]{1,2,0:T(1,128)S(1)} all-gather(s32[8,32,1]{1,2,0:T(1,128)S(1)} %copy-done.2), channel_id=1, replica_groups=mesh['pulse'=4,'range'=4,'tile'=32] {'tile'}, dimensions={0}, use_global_device_ids=true | all-gather | bytes 33792 | tf_op jit(solution)/shard_map/all_gather | solution.py:137
  219.3 5.0 %dynamic-slice_reduce_fusion.2 = s32[256]{0:T(256)S(1)} fusion(s32[256,32,1]{1,2,0:T(1,128)S(1)} %all_gather.18, s32[]{:T(128)S(6)} %select_n.53), kind=kLoop, calls=%fused_computation.65 | loop fusion | bytes 2052 | tf_op jit(solution)/shard_map/jit(dynamic_index_in_dim)/dynamic_slice | solution.py:141
  224.4 1.3 multiply_convert_fusion.1
  225.7 14.6 %reshape.259 = bf16[256,2,64,128]{3,2,1,0:T(8,128)(2,1)} reshape(bf16[256,2,8192]{2,1,0:T(2,128)(2,1)} %all-gather.2.cloned.1.call-done) | data formatting | bytes 16777216 | tf_op jit(solution)/shard_map/reshape | solution.py:68
  240.3 4.2 %convert_bitcast_fusion = bf16[256,2,9,128]{3,2,1,0:T(8,128)(2,1)S(1)} fusion(bf16[256,2,64,128]{3,2,1,0:T(8,128)(2,1)} %reshape.259, s32[256,9]{1,0:T(8,128)S(1)} %iota_add_fusion), kind=kOutput, calls=%fused_computation.26 | convolution fusion | flops 76234752 | bytes 9577472 | tf_op jit(solution)/shard_map/pjk,pckl->pcjl/dot_general | solution.py:73
  245.2 1.3 fusion.24
  246.7 5.1 %fusion.31 = bf16[256,1024]{0,1:T(8,128)(2,1)S(1)} fusion(f32[256,2,1024]{0,2,1:T(8,128)S(1)} %bitcast.71, s32[1024]{0:T(1024)S(1)} %iota_add_fusion.1, s32[256]{0:T(256)S(1)} %get-tuple-element.116), kind=kLoop, calls=%fused_computation.42 | loop fusion | flops 4718592 | bytes 2626560 | tf_op jit(solution)/shard_map/squeeze | solution.py:108
  251.7 5.1 %fusion.43 = (bf16[256,1024]{0,1:T(8,128)(2,1)S(1)}, bf16[256,1024]{0,1:T(8,128)(2,1)S(1)}) fusion(f32[256,2,1024]{0,2,1:T(8,128)S(1)} %bitcast.72, s32[1024]{0:T(1024)S(1)} %iota_add_fusion.1, s32[256]{0:T(256)S(1)} %get-tuple-element.116), kind=kLoop, calls=%fused_computation.75 | loop fusion | flops 5505024 | bytes 3150848 | tf_op jit(solution)/shard_map/neg | solution.py:111
  256.8 2.1 fusion.9
  258.9 55.8 %reduce-scatter.2.cloned.1.call-done = f32[64,2048]{1,0:T(8,128)} async-done(((f32[256,2048]{1,0:T(8,128)}), f32[64,2048]{1,0:T(8,128)}) %reduce-scatter.2.cloned.1.call-update) | async-done | bytes 524304 | tf_op jit(solution)/shard_map/reduce_scatter | solution.py:153
  314.7 1.9 copy.49
  (298 shorter events, 29.2 us)
Async XLA Ops:
  6.5 238.6 %copy-start = (bf16[8,256,128]{2,1,0:T(8,128)(2,1)S(1)}, bf16[8,256,128]{2,1,0:T(8,128)(2,1)}, u32[]{:S(2)}) copy-start(bf16[8,256,128]{2,1,0:T(8,128)(2,1)} %param.11) | copy-start | bytes 1572868
  6.5 219.2 %all-gather.2.cloned.1.call-start = ((), (), s32[]{:S(2)}) async-start(), calls=%async_computation.1 | async-start | bytes 8650752 | tf_op jit(solution)/shard_map/all_gather | solution.py:136
  7.5 6.8 %collective-permute-start.1 = (bf16[2,8,2048]{2,1,0:T(8,128)(2,1)S(1)}, bf16[2,8,2048]{2,1,0:T(8,128)(2,1)S(1)}, u32[]{:S(2)}, u32[]{:S(2)}) collective-permute-start(bf16[2,8,2048]{2,1,0:T(8,128)(2,1)S(1)} %get-tuple-element.127), channel_id=1, source_target_pairs={{32,0},{64,32},{96,64},{33,1},{65,33},{97,65},{34,2},{66,34},{98,6... | collective-permute-start | bytes 196616 | tf_op jit(solution)/shard_map/ppermute | solution.py:20
  8.8 6.0 %collective-permute-start = (bf16[2,8,2048]{2,1,0:T(8,128)(2,1)S(1)}, bf16[2,8,2048]{2,1,0:T(8,128)(2,1)S(1)}, u32[]{:S(2)}, u32[]{:S(2)}) collective-permute-start(bf16[2,8,2048]{2,1,0:T(8,128)(2,1)S(1)} %get-tuple-element.126), channel_id=1, source_target_pairs={{0,32},{32,64},{64,96},{1,33},{33,65},{65,97},{2,34},{34,66},{66,9... | collective-permute-start | bytes 196616 | tf_op jit(solution)/shard_map/ppermute | solution.py:18
  61.1 2.9 copy-start.3
  61.1 3.1 copy-start.4
  61.1 29.9 %copy-start.1 = (s32[8,32]{1,0:T(8,128)S(1)}, s32[8,32]{1,0:T(8,128)}, u32[]{:S(2)}) copy-start(s32[8,32]{1,0:T(8,128)} %param.13) | copy-start | bytes 3076
  61.1 83.8 %copy-start.2 = (s32[8,32,1]{1,2,0:T(1,128)S(1)}, s32[8,32,1]{1,2,0:T(1,128)}, u32[]{:S(2)}) copy-start(s32[8,32,1]{1,2,0:T(1,128)} %param.12) | copy-start | bytes 3076
  62.1 252.6 %reduce-scatter.2.cloned.1.call-start = ((), (), s32[]{:S(2)}) async-start(), calls=%async_computation.2 | async-start | bytes 2621440 | tf_op jit(solution)/shard_map/reduce_scatter | solution.py:153
Sparse Core Ops, SparseCore 0:
  62.2 145.3 all-gather.1
  259.0 55.6 reduce-scatter.1
where the time goes:
time: 324 us; the launch traced here: 323 us
  blocking collectives  155 us (48%)
  local copies, waits for them, and re-layouts  61.7 us (19%)
  waiting for transfers between devices  56.3 us (17%)
  matrix products  14.5 us (4%)
  between operations  14.2 us (4%)
  other arithmetic  13.9 us (4%)
  starting transfers between devices  6 us (2%)
    all_gather x1, blocking collectives, local(): starts_in = lax.all_gather(band_start, 'tile', axis=0, tiled=True)  74.4 us
    reduce_scatter x1, waiting for transfers between devices, local(): lax.psum_scatter(partial_image, 'pulse', scatter_dimension=0, tiled=True)  55.8 us
    all_gather x1, blocking collectives, local(): flags_in = lax.all_gather(visible, 'tile', axis=0, tiled=True)  53.7 us
    unnamed x1, blocking collectives  26.6 us
    another operation x68, local copies, waits for them, and re-layouts, toeplitz_block(): repeated = jnp.tile(segment, block_width)[:2 * block_width * block_width]  21.6 us
    reshape x1, local copies, waits for them, and re-layouts, select_bands(): pieces = signals.reshape(pulses, 2, block_total, line_block)  14.6 us
    dot_general x17, matrix products, add_turn(): return running + jnp.dot(window, matrix, preferred_element_type=jnp.float32)  6.84 us
  transfers between devices with their start and end apart: 4, of which 2 were waited for; matrix products, arithmetic and copies ran while one was open for 3% of the time, Pallas kernels for 0%

commit v1 on v0

--- a/solution.py
+++ b/solution.py
@@ -134,7 +134,8 @@
     empty_index = jnp.zeros((group_pulses,), jnp.int32)
     first_row = jnp.int32(0)
     signals = lax.all_gather(compressed, "tile", axis=0, tiled=True)
-    starts_in = lax.all_gather(band_start, "tile", axis=0, tiled=True)
+    stack = jnp.stack([band_start] * lax.axis_size("tile"))
+    starts_in = jnp.concatenate(lax.all_to_all(stack, "tile", 0, 0), axis=0)
     flags_in = lax.all_gather(visible, "tile", axis=0, tiled=True)
     doppler_in = lax.all_gather(doppler, "tile", axis=0, tiled=True)
     steps_in = lax.all_gather(range_step, "tile", axis=0, tiled=True)

time: 324 us -> 300 us (0.926)
  blocking collectives: 155 us -> 87.1 us
  waiting for transfers between devices: 56.3 us -> 82.2 us
  starting transfers between devices: 6 us -> 25.7 us
  local copies, waits for them, and re-layouts: 61.7 us -> 58.2 us
    all_gather x1 -> x0, blocking collectives: 74.4 us -> none  [local(): starts_in = lax.all_gather(band_start, 'tile', axis=0, tiled=True)]
    all_gather x1, waiting for transfers between devices: 0.02 us -> 29.2 us  [local(): signals = lax.all_gather(compressed, 'tile', axis=0, tiled=True)]
    all_to_all x0 -> x1, starting transfers between devices: none -> 19.7 us  [local(): starts_in = jnp.concatenate(lax.all_to_all(stack, 'tile', 0, 0), axis=0)]
    all_gather x1, blocking collectives: 53.7 us -> 64.1 us  [local(): flags_in = lax.all_gather(visible, 'tile', axis=0, tiled=True)]
    dynamic_slice x1 -> x0, local copies, waits for them, and re-layouts: 4.96 us -> none  [local(): lax.dynamic_index_in_dim(starts_in[:, :, 0], tile_number, 1, keepdims=False)]
    unnamed x1, blocking collectives: 26.6 us -> 22.9 us
    reduce_scatter x1, waiting for transfers between devices: 55.8 us -> 52.5 us  [local(): lax.psum_scatter(partial_image, 'pulse', scatter_dimension=0, tiled=True)]
  transfers between devices with their start and end apart: 4 -> 5, of which waited for: 2 -> 3; matrix products, arithmetic and copies ran while one was open for 3% -> 2% of each run, Pallas kernels for 0% -> 0%
where the time goes in v1:
time: 300 us; the launch traced here: 299 us
  blocking collectives  87.1 us (29%)
  waiting for transfers between devices  82.2 us (27%)
  local copies, waits for them, and re-layouts  58.2 us (19%)
  starting transfers between devices  25.7 us (9%)
  other arithmetic  14.8 us (5%)
  matrix products  14.5 us (5%)
  between operations  14.4 us (5%)
    all_gather x1, blocking collectives, local(): flags_in = lax.all_gather(visible, 'tile', axis=0, tiled=True)  64.1 us
    reduce_scatter x1, waiting for transfers between devices, local(): lax.psum_scatter(partial_image, 'pulse', scatter_dimension=0, tiled=True)  52.5 us
    all_gather x1, waiting for transfers between devices, local(): signals = lax.all_gather(compressed, 'tile', axis=0, tiled=True)  29.2 us
    unnamed x1, blocking collectives  22.9 us
    another operation x68, local copies, waits for them, and re-layouts, toeplitz_block(): repeated = jnp.tile(segment, block_width)[:2 * block_width * block_width]  21.6 us
    all_to_all x1, starting transfers between devices, local(): starts_in = jnp.concatenate(lax.all_to_all(stack, 'tile', 0, 0), axis=0)  19.7 us
    reshape x1, local copies, waits for them, and re-layouts, select_bands(): pieces = signals.reshape(pulses, 2, block_total, line_block)  14.6 us
    dot_general x17, matrix products, add_turn(): return running + jnp.dot(window, matrix, preferred_element_type=jnp.float32)  6.84 us
  transfers between devices with their start and end apart: 5, of which 3 were waited for; matrix products, arithmetic and copies ran while one was open for 2% of the time, Pallas kernels for 0%

profile of v1, /device:TPU:1, one launch (start us, length us, event | category | flops | bytes accessed | tf_op | source)
XLA Modules:
  0.0 298.9 jit_solution(12717202278375032453)
XLA Ops:
  6.5 0.9 fusion.50
  7.5 1.3 collective-permute-start.1
  8.8 4.7 %collective-permute-start = (bf16[2,8,2048]{2,1,0:T(8,128)(2,1)S(1)}, bf16[2,8,2048]{2,1,0:T(8,128)(2,1)S(1)}, u32[]{:S(2)}, u32[]{:S(2)}) collective-permute-start(bf16[2,8,2048]{2,1,0:T(8,128)(2,1)S(1)} %get-tuple-element.126), channel_id=1, source_target_pairs={{0,32},{32,64},{64,96},{1,33},{33,65},{65,97},{2,34},{34,66},{66,9... | collective-permute-start | bytes 196616 | tf_op jit(solution)/shard_map/ppermute | solution.py:18
  13.5 0.7 maximum_maximum_fusion
  14.8 1.0 pad_maximum_fusion.1
  15.8 45.2 %while.14 = (s32[]{:T(128)}, f32[256,512]{1,0:T(8,128)S(1)}, bf16[8,48,2,256]{3,1,0,2:T(8,128)(2,1)S(1)}, bf16[2,4609]{1,0:T(2,128)(2,1)S(1)}, s32[]{:T(128)}, /*index=5*/s32[]{:T(128)}, s32[]{:T(128)}, s32[]{:T(128)}) while((s32[]{:T(128)}, f32[256,512]{1,0:T(8,128)S(1)}, bf16[8,48,2,256]{3,1,0,2:T(8,128)(2,1)S(1)}, ...), condition=%wide.region_1.0_spmd.clone, body=%wide.region_0.0_spmd.clone.sunk | while | flops 136642560 | bytes 7779505 | solution.py:59
  16.4 0.6 tile.65
  17.2 0.6 tile.67
  19.0 0.6 tile.65
  19.9 0.6 tile.67
  21.7 0.6 tile.65
  22.6 0.6 tile.67
  24.4 0.6 tile.65
  25.2 0.6 tile.67
  27.0 0.6 tile.65
  27.9 0.6 tile.67
  29.7 0.6 tile.65
  30.5 0.6 tile.67
  32.3 0.6 tile.65
  33.2 0.6 tile.67
  35.0 0.6 tile.65
  35.9 0.6 tile.67
  37.7 0.6 tile.65
  43.0 0.6 tile.65
  43.8 0.6 tile.67
  45.6 0.6 tile.65
  49.2 0.6 tile.67
  51.0 0.6 tile.65
  51.8 0.6 tile.67
  57.1 0.6 tile.67
  58.9 0.6 tile.65
  61.3 0.8 convert_element_type.58
  62.1 0.7 reshape.227
  62.8 19.7 %all-to-all-start = ((s32[32,1,256]{2,1,0:T(1,128)}), s32[32,1,256]{2,1,0:T(1,128)S(1)}, u32[]{:S(2)}, u32[]{:S(2)}) async-start(s32[32,1,256]{2,1,0:T(1,128)} %reshape.227), calls=%async_computation | async-start | bytes 65536 | tf_op jit(solution)/shard_map/all_to_all | solution.py:138
  82.6 1.3 dynamic-slice.6
  85.1 22.9 %all-reduce.2 = (s32[256]{0:T(256)S(1)}, s32[256]{0:T(256)S(1)}) all-reduce(s32[256]{0:T(256)S(1)} %dynamic-update-slice.1, s32[256]{0:T(256)S(1)} %dynamic-update-slice), channel_id=1, replica_groups=mesh['pulse'=4,'range'=4,'tile'=32] {'tile'}, use_global_device_ids=true, to_apply=%add.1 | all-reduce | flops 512 | bytes 4096
  108.0 64.1 %all_gather.13 = s32[256,32]{1,0:T(8,128)S(1)} all-gather(s32[8,32]{1,0:T(8,128)S(1)} %copy-done.2), channel_id=1, replica_groups=mesh['pulse'=4,'range'=4,'tile'=32] {'tile'}, dimensions={0}, use_global_device_ids=true | all-gather | bytes 33792 | tf_op jit(solution)/shard_map/all_gather | solution.py:139
  172.3 1.3 multiply_convert_fusion.1
  174.2 0.7 reduce.8
  175.3 29.2 %all-gather.2.cloned.1.call-done = bf16[256,2,8192]{2,1,0:T(2,128)(2,1)} async-done(((bf16[8,2,8192]{2,1,0:T(2,128)(2,1)}), bf16[256,2,8192]{2,1,0:T(2,128)(2,1)}) %all-gather.2.cloned.1.call-update) | async-done | bytes 8388624 | tf_op jit(solution)/shard_map/all_gather | solution.py:136
  204.5 14.6 %reshape.204 = bf16[256,2,64,128]{3,2,1,0:T(8,128)(2,1)} reshape(bf16[256,2,8192]{2,1,0:T(2,128)(2,1)} %all-gather.2.cloned.1.call-done) | data formatting | bytes 16777216 | tf_op jit(solution)/shard_map/reshape | solution.py:68
  219.1 4.2 %convert_bitcast_fusion = bf16[256,2,9,128]{3,2,1,0:T(8,128)(2,1)S(1)} fusion(bf16[256,2,64,128]{3,2,1,0:T(8,128)(2,1)} %reshape.204, s32[256,9]{1,0:T(8,128)S(1)} %iota_add_fusion), kind=kOutput, calls=%fused_computation.26 | convolution fusion | flops 76234752 | bytes 9577472 | tf_op jit(solution)/shard_map/pjk,pckl->pcjl/dot_general | solution.py:73
  224.0 1.3 fusion.24
  225.5 5.1 %fusion.31 = bf16[256,1024]{0,1:T(8,128)(2,1)S(1)} fusion(f32[256,2,1024]{0,2,1:T(8,128)S(1)} %bitcast.78, s32[1024]{0:T(1024)S(1)} %iota_add_fusion.1, s32[256]{0:T(256)S(1)} %get-tuple-element.116), kind=kLoop, calls=%fused_computation.42 | loop fusion | flops 4718592 | bytes 2626560 | tf_op jit(solution)/shard_map/squeeze | solution.py:108
  230.6 5.1 %fusion.46 = (bf16[256,1024]{0,1:T(8,128)(2,1)S(1)}, bf16[256,1024]{0,1:T(8,128)(2,1)S(1)}) fusion(f32[256,2,1024]{0,2,1:T(8,128)S(1)} %bitcast.79, s32[1024]{0:T(1024)S(1)} %iota_add_fusion.1, s32[256]{0:T(256)S(1)} %get-tuple-element.116), kind=kLoop, calls=%fused_computation.78 | loop fusion | flops 5505024 | bytes 3150848 | tf_op jit(solution)/shard_map/neg | solution.py:111
  235.7 2.1 fusion.9
  237.8 52.5 %reduce-scatter.2.cloned.1.call-done = f32[64,2048]{1,0:T(8,128)} async-done(((f32[256,2048]{1,0:T(8,128)}), f32[64,2048]{1,0:T(8,128)}) %reduce-scatter.2.cloned.1.call-update) | async-done | bytes 524304 | tf_op jit(solution)/shard_map/reduce_scatter | solution.py:154
  290.2 1.9 copy.49
  (304 shorter events, 31.2 us)
Async XLA Ops:
  6.5 217.5 %copy-start = (bf16[8,256,128]{2,1,0:T(8,128)(2,1)S(1)}, bf16[8,256,128]{2,1,0:T(8,128)(2,1)}, u32[]{:S(2)}) copy-start(bf16[8,256,128]{2,1,0:T(8,128)(2,1)} %param.11) | copy-start | bytes 1572868
  6.5 198.0 %all-gather.2.cloned.1.call-start = ((), (), s32[]{:S(2)}) async-start(), calls=%async_computation.2 | async-start | bytes 8650752 | tf_op jit(solution)/shard_map/all_gather | solution.py:136
  7.5 6.8 %collective-permute-start.1 = (bf16[2,8,2048]{2,1,0:T(8,128)(2,1)S(1)}, bf16[2,8,2048]{2,1,0:T(8,128)(2,1)S(1)}, u32[]{:S(2)}, u32[]{:S(2)}) collective-permute-start(bf16[2,8,2048]{2,1,0:T(8,128)(2,1)S(1)} %get-tuple-element.127), channel_id=1, source_target_pairs={{32,0},{64,32},{96,64},{33,1},{65,33},{97,65},{34,2},{66,34},{98,6... | collective-permute-start | bytes 196616 | tf_op jit(solution)/shard_map/ppermute | solution.py:20
  8.8 6.0 %collective-permute-start = (bf16[2,8,2048]{2,1,0:T(8,128)(2,1)S(1)}, bf16[2,8,2048]{2,1,0:T(8,128)(2,1)S(1)}, u32[]{:S(2)}, u32[]{:S(2)}) collective-permute-start(bf16[2,8,2048]{2,1,0:T(8,128)(2,1)S(1)} %get-tuple-element.126), channel_id=1, source_target_pairs={{0,32},{32,64},{64,96},{1,33},{33,65},{65,97},{2,34},{34,66},{66,9... | collective-permute-start | bytes 196616 | tf_op jit(solution)/shard_map/ppermute | solution.py:18
  61.1 1.0 copy-start.1
  61.1 23.5 %copy-start.3 = (s32[8]{0:T(128)S(1)}, s32[8]{0:T(128)}, u32[]{:S(2)}) copy-start(s32[8]{0:T(128)} %param.15) | copy-start | bytes 100
  61.1 23.8 %copy-start.4 = (s32[8]{0:T(128)S(1)}, s32[8]{0:T(128)}, u32[]{:S(2)}) copy-start(s32[8]{0:T(128)} %param.14) | copy-start | bytes 100
  61.1 46.9 %copy-start.2 = (s32[8,32]{1,0:T(8,128)S(1)}, s32[8,32]{1,0:T(8,128)}, u32[]{:S(2)}) copy-start(s32[8,32]{1,0:T(8,128)} %param.13) | copy-start | bytes 3076
  62.8 110.8 %all-to-all-start = ((s32[32,1,256]{2,1,0:T(1,128)}), s32[32,1,256]{2,1,0:T(1,128)S(1)}, u32[]{:S(2)}, u32[]{:S(2)}) async-start(s32[32,1,256]{2,1,0:T(1,128)} %reshape.227), calls=%async_computation | async-start | bytes 65536 | tf_op jit(solution)/shard_map/all_to_all | solution.py:138
  82.5 207.7 %reduce-scatter.2.cloned.1.call-start = ((), (), s32[]{:S(2)}) async-start(), calls=%async_computation.3 | async-start | bytes 2621440 | tf_op jit(solution)/shard_map/reduce_scatter | solution.py:154
Sparse Core Ops, SparseCore 0:
  62.2 142.2 all-gather.1
  237.9 52.2 reduce-scatter.1
